TPU v7x, 512 devices: a whole 4x4x16 slice. The times are simulated.
512 devices in a mesh: space: 32 (over z, x_lo), chan: 16 (over x_hi, y, core).
Axes of the slice: x: 4 (x_hi: 2, x_lo: 2; x = x_hi * 2 + x_lo), y: 4, z: 16, core: 2. Of those that a mesh axis runs over, the one named last changes fastest.
Arguments:
- volume: bfloat16 [64, 256, 8, 128], P('space', 'chan'), may hold values from -6 to 6
- kernel: bfloat16 [27, 256, 256], P(None, 'chan'), may hold values from -0.078125 to 0.078125
- cotangent: bfloat16 [64, 256, 8, 128], P('space', 'chan'), may hold values from -6 to 6
Outputs:
- output_map: bfloat16 [64, 256, 8, 128], P('space', 'chan')
- input_grad: bfloat16 [64, 256, 8, 128], P('space', 'chan')
- kernel_grad: float32 [27, 256, 256], P(None, 'chan')
All inputs are finite; a program needn't handle non-finite values.
Results may differ from a plain program's by a relative error of at most 0.001.
Values may be sent and summed in bfloat16 or wider, within the bound.
A program may use at most 128 MiB of HBM per device.

v0:
```python
import math
import jax
import jax.numpy as jnp
from jax import lax
from jax.sharding import PartitionSpec as P


def with_halo(block, sides, width):
    for axis, dim in sides:
        count = lax.axis_size(axis)
        forward = [(i, i + 1) for i in range(count - 1)]
        backward = [(target, source) for source, target in forward]
        low = lax.ppermute(
            lax.slice_in_dim(block, block.shape[dim] - width, None, axis=dim), axis, forward
        )
        high = lax.ppermute(lax.slice_in_dim(block, 0, width, axis=dim), axis, backward)
        block = jnp.concatenate([low, block, high], axis=dim)
    return block


def plane_stack(piece, height, width, flipped):
    cells = height * width
    padded = jnp.pad(piece, ((0, 0), (0, 0), (width + 1, width + 1)))
    column = lax.broadcasted_iota(jnp.int32, (1, 1, cells), 2) % width
    windows = []
    for row_step in range(3):
        for col_step in range(3):
            row_from = 2 - row_step if flipped else row_step
            col_from = 2 - col_step if flipped else col_step
            offset = width + 1 + (row_from - 1) * width + (col_from - 1)
            shifted = padded[:, :, offset : offset + cells]
            target = column + (col_from - 1)
            inside = ((target >= 0) & (target < width)).astype(piece.dtype)
            windows.append(shifted * inside)
    return jnp.concatenate(windows, axis=1)


def on_device(volume, kernel, cotangent):
    depth, chans_local, height, width = volume.shape
    filters_local = cotangent.shape[1]
    cells = height * width
    scale_factor = 1.0 / math.sqrt(depth * lax.axis_size("space") * height * width)
    volume_flat = volume.reshape(depth, chans_local, cells)
    grad_flat = cotangent.reshape(depth, filters_local, cells)
    columns = lax.all_to_all(kernel, "chan", split_axis=2, concat_axis=1, tiled=True)
    init_output = jnp.zeros((depth, filters_local, cells), jnp.float32)
    init_input = jnp.zeros((depth, chans_local, cells), jnp.float32)
    rims = with_halo(volume_flat, (("space", 0),), 1)
    piece = lax.all_gather(rims, "chan", axis=1, tiled=True)
    output_acc = init_output
    count = piece.shape[1]
    stacked = plane_stack(piece, height, width, False)
    grads = []
    for depth_step in range(3):
        window = stacked[depth_step : depth_step + depth]
        taps = kernel[9 * depth_step : 9 * depth_step + 9]
        weights = jnp.transpose(taps, (1, 0, 2)).reshape(filters_local, 9 * count)
        output_acc = output_acc + jnp.einsum(
            "fj,zjp->zfp", weights, window, preferred_element_type=jnp.float32
        )
        term = jnp.einsum("zfp,zjp->fj", grad_flat, window, preferred_element_type=jnp.float32)
        grads.append(jnp.transpose(term.reshape(filters_local, 9, count), (1, 0, 2)))
    kernel_acc = jnp.concatenate(grads, axis=0)
    output_acc, kernel_acc = (output_acc, kernel_acc)
    grad_ext = with_halo(grad_flat, (("space", 0),), 1)
    total = init_input
    piece = lax.all_gather(grad_ext, "chan", axis=1, tiled=True)
    count = piece.shape[1]
    stacked = plane_stack(piece, height, width, True)
    for depth_step in range(3):
        window = stacked[2 - depth_step : 2 - depth_step + depth]
        taps = columns[9 * depth_step : 9 * depth_step + 9]
        weights = jnp.transpose(taps, (2, 0, 1)).reshape(chans_local, 9 * count)
        total = total + jnp.einsum(
            "kj,zjp->zkp", weights, window, preferred_element_type=jnp.float32
        )
    kernel_grad = lax.psum(kernel_acc, "space") * scale_factor
    output_map = output_acc.astype(jnp.bfloat16).reshape(depth, filters_local, height, width)
    input_grad = total.astype(jnp.bfloat16).reshape(depth, chans_local, height, width)
    return (output_map, input_grad, kernel_grad)


def solution(mesh):
    return jax.shard_map(
        on_device,
        mesh=mesh,
        in_specs=(
            P("space", "chan", None, None),
            P(None, "chan", None),
            P("space", "chan", None, None),
        ),
        out_specs=(
            P("space", "chan", None, None),
            P("space", "chan", None, None),
            P(None, "chan", None),
        ),
        check_vma=False,
    )
```

profile of v0, /device:TPU:8, one launch (start us, length us, event | category | flops | bytes accessed | tf_op | source)
XLA Modules:
  0.0 456.1 jit_solution(4387820770311451748)
XLA Ops:
  8.1 3.4 collective-permute-start.2
  13.7 3.6 collective-permute-done.3
  18.9 4.7 %collective-permute-start = (bf16[1,16,1024]{2,1,0:T(8,128)(2,1)S(1)}, bf16[1,16,1024]{2,1,0:T(8,128)(2,1)S(1)}, u32[]{:S(2)}, u32[]{:S(2)}) collective-permute-start(bf16[1,16,1024]{2,1,0:T(8,128)(2,1)S(1)} %slice.120), channel_id=1, source_target_pairs={{0,16},{16,32},{32,48},{48,64},{64,80},{80,96},{96,112},{112,128},... | collective-permute-start | bytes 98312 | tf_op jit(solution)/shard_map/ppermute | solution.py:13
  25.8 3.6 collective-permute-done.1
  32.1 2.5 reshape.125
  34.6 7.4 %all-to-all-start = ((bf16[16,2,3456]{2,1,0:T(2,128)(2,1)}), bf16[16,2,3456]{2,1,0:T(2,128)(2,1)S(1)}, u32[]{:S(2)}, u32[]{:S(2)}) async-start(bf16[16,2,3456]{2,1,0:T(2,128)(2,1)} %reshape.125), calls=%async_computation | async-start | bytes 442368 | tf_op jit(solution)/shard_map/all_to_all | solution.py:45
  44.3 5.4 %all-to-all-done = bf16[16,2,3456]{2,1,0:T(2,128)(2,1)S(1)} async-done(((bf16[16,2,3456]{2,1,0:T(2,128)(2,1)}), bf16[16,2,3456]{2,1,0:T(2,128)(2,1)S(1)}, u32[]{:S(2)}, u32[]{:S(2)}) %all-to-all-start) | async-done | bytes 221216 | tf_op jit(solution)/shard_map/all_to_all | solution.py:45
  49.6 2.7 reshape.126
  52.3 4.2 copy.49
  61.3 26.4 %all-gather.5.cloned.1.call-done = bf16[4,256,1024]{2,1,0:T(8,128)(2,1)} async-done(((bf16[4,16,1024]{2,1,0:T(8,128)(2,1)}), bf16[4,256,1024]{2,1,0:T(8,128)(2,1)}) %all-gather.5.cloned.1.call-update) | async-done | bytes 2097168 | tf_op jit(solution)/shard_map/all_gather | solution.py:67
  87.7 3.8 fusion.29
  93.3 2.6 fusion.33
  95.9 2.6 fusion.35
  100.4 52.5 %all-gather.3.cloned.1.call-done = bf16[4,256,1024]{2,1,0:T(8,128)(2,1)} async-done(((bf16[4,16,1024]{2,1,0:T(8,128)(2,1)}), bf16[4,256,1024]{2,1,0:T(8,128)(2,1)}) %all-gather.3.cloned.1.call-update) | async-done | bytes 2097168 | tf_op jit(solution)/shard_map/all_gather | solution.py:49
  152.9 4.5 fusion.37
  157.3 2.7 fusion.39
  163.7 3.9 fusion.43
  172.4 2.5 convolution_bitcast_fusion.2
  175.0 2.8 convolution_bitcast_fusion.1
  178.8 2.5 convolution_bitcast_fusion
  182.4 5.0 %fusion = f32[2,1024,16]{1,2,0:T(8,128)S(1)} fusion(bf16[16,2304,1]{1,0,2:T(8,128)(2,1)S(1)} %reshape.115, bf16[4,2304,1024]{2,1,0:T(8,128)(2,1)} %get-tuple-element.22), kind=kOutput, calls=%fused_computation | convolution fusion | flops 150994944 | bytes 9641984 | tf_op jit(solution)/shard_map/kj,zjp->zkp/dot_general | solution.py:74
  187.4 5.2 %fusion.2 = f32[2,1024,16]{1,2,0:T(8,128)S(1)} fusion(bf16[16,2304,1]{1,0,2:T(8,128)(2,1)S(1)} %reshape.114, bf16[4,2304,1024]{2,1,0:T(8,128)(2,1)} %get-tuple-element.22), kind=kOutput, calls=%fused_computation.2 | convolution fusion | flops 150994944 | bytes 9641984 | tf_op jit(solution)/shard_map/kj,zjp->zkp/dot_general | solution.py:74
  192.6 5.8 %fusion.56 = bf16[2,1024,16]{1,2,0:T(8,128)(2,1)S(1)} fusion(f32[2,1024,16]{1,2,0:T(8,128)S(1)} %fusion, f32[2,1024,16]{1,2,0:T(8,128)S(1)} %fusion.2, bf16[16,2304,1]{1,0,2:T(8,128)(2,1)S(1)} %reshape.113, bf16[4,2304,1024]{2,1,0:T(8,128)(2,1)} %get-tuple-element.22), kind=kOutput, calls=%fused_computation.69 | convolution fusion | flops 151093248 | bytes 9838592 | tf_op jit(solution)/shard_map/kj,zjp->zkp/dot_general | solution.py:74
  204.0 243.3 %all-reduce.4.cloned.1.call-done = f32[27,16,256]{2,0,1:T(8,128)} async-done(((f32[27,16,256]{2,0,1:T(8,128)}), f32[27,16,256]{2,0,1:T(8,128)}) %all-reduce.4.cloned.1.call-update) | async-done | bytes 442384 | tf_op jit(solution)/shard_map/psum | solution.py:77
  (84 shorter events, 38.3 us)
Async XLA Ops:
  7.2 34.9 %copy-start.6 = (bf16[27,16,256]{2,1,0:T(8,128)(2,1)S(1)}, bf16[27,16,256]{2,1,0:T(8,128)(2,1)}, u32[]{:S(2)}) copy-start(bf16[27,16,256]{2,1,0:T(8,128)(2,1)} %param.4) | copy-start | bytes 663556
  7.2 80.5 %all-gather.5.cloned.1.call-start = ((), (), s32[]{:S(2)}) async-start(), calls=%async_computation.2 | async-start | bytes 2228224 | tf_op jit(solution)/shard_map/all_gather | solution.py:67
  8.1 5.6 %collective-permute-start.2 = (bf16[1,16,1024]{2,1,0:T(8,128)(2,1)S(1)}, bf16[1,16,1024]{2,1,0:T(8,128)(2,1)S(1)}, u32[]{:S(2)}, u32[]{:S(2)}) collective-permute-start(bf16[1,16,1024]{2,1,0:T(8,128)(2,1)S(1)} %slice.138), channel_id=1, source_target_pairs={{0,16},{16,32},{32,48},{48,64},{64,80},{80,96},{96,112},{112,128},... | collective-permute-start | bytes 98312 | tf_op jit(solution)/shard_map/ppermute | solution.py:13
  11.5 5.8 %collective-permute-start.3 = (bf16[1,16,1024]{2,1,0:T(8,128)(2,1)S(1)}, bf16[1,16,1024]{2,1,0:T(8,128)(2,1)S(1)}, u32[]{:S(2)}, u32[]{:S(2)}) collective-permute-start(bf16[1,16,1024]{2,1,0:T(8,128)(2,1)S(1)} %slice.140), channel_id=1, source_target_pairs={{16,0},{32,16},{48,32},{64,48},{80,64},{96,80},{112,96},{128,112},... | collective-permute-start | bytes 98312 | tf_op jit(solution)/shard_map/ppermute | solution.py:16
  13.7 16.4 %copy-start.4 = (bf16[2,16,1024]{2,1,0:T(8,128)(2,1)}, bf16[2,16,1024]{2,1,0:T(8,128)(2,1)S(1)}, u32[]{:S(2)}) copy-start(bf16[2,16,1024]{2,1,0:T(8,128)(2,1)S(1)} %reshape.102) | copy-start | bytes 196612
  18.0 134.9 %all-gather.3.cloned.1.call-start = ((), (), s32[]{:S(2)}) async-start(), calls=%async_computation.1 | async-start | bytes 2228224 | tf_op jit(solution)/shard_map/all_gather | solution.py:49
  18.9 6.9 %collective-permute-start = (bf16[1,16,1024]{2,1,0:T(8,128)(2,1)S(1)}, bf16[1,16,1024]{2,1,0:T(8,128)(2,1)S(1)}, u32[]{:S(2)}, u32[]{:S(2)}) collective-permute-start(bf16[1,16,1024]{2,1,0:T(8,128)(2,1)S(1)} %slice.120), channel_id=1, source_target_pairs={{0,16},{16,32},{32,48},{48,64},{64,80},{80,96},{96,112},{112,128},... | collective-permute-start | bytes 98312 | tf_op jit(solution)/shard_map/ppermute | solution.py:13
  23.6 5.8 %collective-permute-start.1 = (bf16[1,16,1024]{2,1,0:T(8,128)(2,1)S(1)}, bf16[1,16,1024]{2,1,0:T(8,128)(2,1)S(1)}, u32[]{:S(2)}, u32[]{:S(2)}) collective-permute-start(bf16[1,16,1024]{2,1,0:T(8,128)(2,1)S(1)} %slice.122), channel_id=1, source_target_pairs={{16,0},{32,16},{48,32},{64,48},{80,64},{96,80},{112,96},{128,112},... | collective-permute-start | bytes 98312 | tf_op jit(solution)/shard_map/ppermute | solution.py:16
  34.6 15.0 %all-to-all-start = ((bf16[16,2,3456]{2,1,0:T(2,128)(2,1)}), bf16[16,2,3456]{2,1,0:T(2,128)(2,1)S(1)}, u32[]{:S(2)}, u32[]{:S(2)}) async-start(bf16[16,2,3456]{2,1,0:T(2,128)(2,1)} %reshape.125), calls=%async_computation | async-start | bytes 442368 | tf_op jit(solution)/shard_map/all_to_all | solution.py:45
  42.0 405.2 %all-reduce.4.cloned.1.call-start = ((), (), s32[]{:S(2)}) async-start(), calls=%async_computation.3 | async-start | bytes 1048576 | tf_op jit(solution)/shard_map/psum | solution.py:77
  87.7 3.8 copy-start.2
  157.3 2.7 copy-start.3
  170.8 1.6 copy-start.5
  172.4 6.4 %copy-start = (bf16[4,2304,1024]{2,1,0:T(8,128)(2,1)}, bf16[4,2304,1024]{2,1,0:T(8,128)(2,1)S(1)}, u32[]{:S(2)}) copy-start(bf16[4,2304,1024]{2,1,0:T(8,128)(2,1)S(1)} %fusion.27) | copy-start | bytes 56623108
  187.4 11.8 %copy-start.1 = (bf16[4,2304,1024]{2,1,0:T(8,128)(2,1)S(1)}, bf16[4,2304,1024]{2,1,0:T(8,128)(2,1)}, u32[]{:S(2)}) copy-start(bf16[4,2304,1024]{2,1,0:T(8,128)(2,1)} %copy-done) | copy-start | bytes 56623108
  192.6 6.7 %copy-start.7 = (bf16[16,2304,1]{1,0,2:T(8,128)(2,1)S(1)}, bf16[16,2304,1]{1,0,2:T(8,128)(2,1)}, u32[]{:S(2)}) copy-start(bf16[16,2304,1]{1,0,2:T(8,128)(2,1)} %reshape.111) | copy-start | bytes 221188
  199.3 1.3 copy-start.8
  200.6 1.4 copy-start.9
Sparse Core Ops, SparseCore 0:
  18.1 69.4 all-gather.4
  91.1 61.7 all-gather.2
  182.5 264.7 all-reduce.3
where the time goes:
time: 462 us; the launch traced here: 456 us
  waiting for transfers between devices  335 us (73%)
  other arithmetic  35.5 us (8%)
  matrix products  27.8 us (6%)
  local copies, waits for them, and re-layouts  25.5 us (6%)
  starting transfers between devices  18.2 us (4%)
  between operations  14.3 us (3%)
    psum x1, waiting for transfers between devices, on_device(): kernel_grad = lax.psum(kernel_acc, 'space') * scale_factor  243 us
    all_gather x1, waiting for transfers between devices, on_device(): piece = lax.all_gather(rims, 'chan', axis=1, tiled=True)  52.5 us
    unnamed x13, other arithmetic  27.2 us
    all_gather x1, waiting for transfers between devices, on_device(): piece = lax.all_gather(grad_ext, 'chan', axis=1, tiled=True)  26.4 us
    dot_general x3, matrix products, on_device(): jnp.einsum('kj,zjp->zkp', weights, window, preferred_element_type=jnp.flo...  16 us
    unnamed x26, local copies, waits for them, and re-layouts  10.9 us
  transfers between devices with their start and end apart: 8, of which 6 were waited for; matrix products, arithmetic and copies ran while one was open for 12% of the time, Pallas kernels for 0%

commit v1 on v0

--- a/solution.py
+++ b/solution.py
@@ -46,7 +46,9 @@
     init_output = jnp.zeros((depth, filters_local, cells), jnp.float32)
     init_input = jnp.zeros((depth, chans_local, cells), jnp.float32)
     rims = with_halo(volume_flat, (("space", 0),), 1)
-    piece = lax.all_gather(rims, "chan", axis=1, tiled=True)
+    piece = jnp.concatenate(
+        lax.all_to_all(jnp.stack([rims] * lax.axis_size("chan")), "chan", 0, 0), axis=1
+    )
     output_acc = init_output
     count = piece.shape[1]
     stacked = plane_stack(piece, height, width, False)

time: 462 us -> 414 us (0.90)
  waiting for transfers between devices: 335 us -> 268 us
  local copies, waits for them, and re-layouts: 25.5 us -> 44.8 us
  other arithmetic: 35.5 us -> 27.2 us
  starting transfers between devices: 18.2 us -> 25.4 us
    all_gather x1 -> x0, waiting for transfers between devices: 52.5 us -> none  [on_device(): piece = lax.all_gather(rims, 'chan', axis=1, tiled=True)]
    all_gather x1, waiting for transfers between devices: 26.4 us -> 4.98 us  [on_device(): piece = lax.all_gather(grad_ext, 'chan', axis=1, tiled=True)]
    all_to_all x0 -> x1, waiting for transfers between devices: none -> 8.87 us  [on_device(): lax.all_to_all(jnp.stack([rims] * lax.axis_size('chan')), 'chan', 0, 0)]
    unnamed x26 -> x28, local copies, waits for them, and re-layouts: 10.9 us -> 19.5 us
    unnamed x13, other arithmetic: 27.2 us -> 19 us
    all_to_all x0 -> x1, starting transfers between devices: none -> 7.83 us  [on_device(): lax.all_to_all(jnp.stack([rims] * lax.axis_size('chan')), 'chan', 0, 0)]
    slice x7, local copies, waits for them, and re-layouts: 4.45 us -> 11.3 us  [on_device(): taps = columns[9 * depth_step:9 * depth_step + 9]]
    all_to_all x1, waiting for transfers between devices: 5.36 us -> 0.01 us  [on_device(): lax.all_to_all(kernel, 'chan', split_axis=2, concat_axis=1, tiled=True)]
  transfers between devices with their start and end apart: 8 -> 8, of which waited for: 6 -> 5; matrix products, arithmetic and copies ran while one was open for 12% -> 13% of each run, Pallas kernels for 0% -> 0%
where the time goes in v1:
time: 414 us; the launch traced here: 408 us
  waiting for transfers between devices  268 us (65%)
  local copies, waits for them, and re-layouts  44.8 us (11%)
  matrix products  27.8 us (7%)
  other arithmetic  27.2 us (7%)
  starting transfers between devices  25.4 us (6%)
  between operations  14.7 us (4%)
    psum x1, waiting for transfers between devices, on_device(): kernel_grad = lax.psum(kernel_acc, 'space') * scale_factor  247 us
    unnamed x28, local copies, waits for them, and re-layouts  19.5 us
    unnamed x13, other arithmetic  19 us
    dot_general x3, matrix products, on_device(): jnp.einsum('kj,zjp->zkp', weights, window, preferred_element_type=jnp.flo...  16 us
    slice x7, local copies, waits for them, and re-layouts, on_device(): taps = columns[9 * depth_step:9 * depth_step + 9]  11.3 us
    all_to_all x1, waiting for transfers between devices, on_device(): lax.all_to_all(jnp.stack([rims] * lax.axis_size('chan')), 'chan', 0, 0)  8.87 us
  transfers between devices with their start and end apart: 8, of which 5 were waited for; matrix products, arithmetic and copies ran while one was open for 13% of the time, Pallas kernels for 0%

profile of v1, /device:TPU:8, one launch (start us, length us, event | category | flops | bytes accessed | tf_op | source)
XLA Modules:
  0.0 407.9 jit_solution(17727695553102807954)
XLA Ops:
  8.0 3.4 collective-permute-start.2
  13.6 3.6 collective-permute-done.3
  20.0 2.5 reshape.135
  22.5 7.3 %all-to-all-start.1 = ((bf16[16,2,3456]{2,1,0:T(2,128)(2,1)}), bf16[16,2,3456]{2,1,0:T(2,128)(2,1)S(1)}, u32[]{:S(2)}, u32[]{:S(2)}) async-start(bf16[16,2,3456]{2,1,0:T(2,128)(2,1)} %reshape.135), calls=%async_computation.1 | async-start | bytes 442368 | tf_op jit(solution)/shard_map/all_to_all | solution.py:45
  30.6 4.2 %collective-permute-start = (bf16[1,16,1024]{2,1,0:T(8,128)(2,1)S(1)}, bf16[1,16,1024]{2,1,0:T(8,128)(2,1)S(1)}, u32[]{:S(2)}, u32[]{:S(2)}) collective-permute-start(bf16[1,16,1024]{2,1,0:T(8,128)(2,1)S(1)} %slice.120), channel_id=1, source_target_pairs={{0,16},{16,32},{32,48},{48,64},{64,80},{80,96},{96,112},{112,128},... | collective-permute-start | bytes 98312 | tf_op jit(solution)/shard_map/ppermute | solution.py:13
  37.0 3.6 collective-permute-done.1
  42.2 7.8 %all-to-all-start = ((bf16[16,4,16,1024]{3,2,1,0:T(8,128)(2,1)}), bf16[16,4,16,1024]{3,2,1,0:T(8,128)(2,1)S(1)}, u32[]{:S(2)}, u32[]{:S(2)}) async-start(bf16[16,4,16,1024]{3,2,1,0:T(8,128)(2,1)} %stack.2), calls=%async_computation | async-start | bytes 4194304 | tf_op jit(solution)/shard_map/all_to_all | solution.py:50
  52.9 3.5 reshape.136
  56.4 4.8 %copy.51 = bf16[27,16,16,16]{3,2,1,0:T(8,128)(2,1)} copy(bf16[27,16,16,16]{0,1,3,2:T(8,128)(2,1)S(1)} %bitcast.88) | data formatting | bytes 442368 | tf_op jit(solution)/shard_map/all_to_all | solution.py:45
  61.2 2.6 fusion.79
  63.9 2.6 copy.48
  72.8 8.9 %all-to-all-done = bf16[16,4,16,1024]{3,2,1,0:T(8,128)(2,1)S(1)} async-done(((bf16[16,4,16,1024]{3,2,1,0:T(8,128)(2,1)}), bf16[16,4,16,1024]{3,2,1,0:T(8,128)(2,1)S(1)}, u32[]{:S(2)}, u32[]{:S(2)}) %all-to-all-start) | async-done | bytes 2097184 | tf_op jit(solution)/shard_map/all_to_all | solution.py:50
  84.8 5.0 %all-gather.2.cloned.1.call-done = bf16[4,256,1024]{2,1,0:T(8,128)(2,1)} async-done(((bf16[4,16,1024]{2,1,0:T(8,128)(2,1)}), bf16[4,256,1024]{2,1,0:T(8,128)(2,1)}) %all-gather.2.cloned.1.call-update) | async-done | bytes 2097168 | tf_op jit(solution)/shard_map/all_gather | solution.py:69
  95.9 6.5 %copy-done.3 = bf16[4,2304,1024]{2,1,0:T(8,128)(2,1)} copy-done((bf16[4,2304,1024]{2,1,0:T(8,128)(2,1)}, bf16[4,2304,1024]{2,1,0:T(8,128)(2,1)S(1)}, u32[]{:S(2)}) %copy-start.3) | copy-done | bytes 18874392
  102.3 3.1 fusion.37
  105.5 2.9 fusion.39
  111.9 3.9 fusion.43
  120.4 2.5 convolution_bitcast_fusion.2
  122.9 2.8 convolution_bitcast_fusion.1
  126.8 2.5 convolution_bitcast_fusion
  130.4 5.0 %fusion = f32[2,1024,16]{1,2,0:T(8,128)S(1)} fusion(bf16[16,2304,1]{1,0,2:T(8,128)(2,1)S(1)} %reshape.125, bf16[4,2304,1024]{2,1,0:T(8,128)(2,1)} %get-tuple-element.22), kind=kOutput, calls=%fused_computation | convolution fusion | flops 150994944 | bytes 9641984 | tf_op jit(solution)/shard_map/kj,zjp->zkp/dot_general | solution.py:76
  135.4 5.2 %fusion.2 = f32[2,1024,16]{1,2,0:T(8,128)S(1)} fusion(bf16[16,2304,1]{1,0,2:T(8,128)(2,1)S(1)} %reshape.124, bf16[4,2304,1024]{2,1,0:T(8,128)(2,1)} %get-tuple-element.22), kind=kOutput, calls=%fused_computation.2 | convolution fusion | flops 150994944 | bytes 9641984 | tf_op jit(solution)/shard_map/kj,zjp->zkp/dot_general | solution.py:76
  140.6 5.8 %fusion.56 = bf16[2,1024,16]{1,2,0:T(8,128)(2,1)S(1)} fusion(f32[2,1024,16]{1,2,0:T(8,128)S(1)} %fusion, f32[2,1024,16]{1,2,0:T(8,128)S(1)} %fusion.2, bf16[16,2304,1]{1,0,2:T(8,128)(2,1)S(1)} %reshape.123, bf16[4,2304,1024]{2,1,0:T(8,128)(2,1)} %get-tuple-element.22), kind=kOutput, calls=%fused_computation.69 | convolution fusion | flops 151093248 | bytes 9838592 | tf_op jit(solution)/shard_map/kj,zjp->zkp/dot_general | solution.py:76
  151.9 246.8 %all-reduce.4.cloned.1.call-done = f32[27,16,256]{2,0,1:T(8,128)} async-done(((f32[27,16,256]{2,0,1:T(8,128)}), f32[27,16,256]{2,0,1:T(8,128)}) %all-reduce.4.cloned.1.call-update) | async-done | bytes 442384 | tf_op jit(solution)/shard_map/psum | solution.py:79
  (87 shorter events, 46.2 us)
Async XLA Ops:
  7.2 82.6 %all-gather.2.cloned.1.call-start = ((), (), s32[]{:S(2)}) async-start(), calls=%async_computation.2 | async-start | bytes 2228224 | tf_op jit(solution)/shard_map/all_gather | solution.py:69
  8.0 5.6 %collective-permute-start.2 = (bf16[1,16,1024]{2,1,0:T(8,128)(2,1)S(1)}, bf16[1,16,1024]{2,1,0:T(8,128)(2,1)S(1)}, u32[]{:S(2)}, u32[]{:S(2)}) collective-permute-start(bf16[1,16,1024]{2,1,0:T(8,128)(2,1)S(1)} %slice.138), channel_id=1, source_target_pairs={{0,16},{16,32},{32,48},{48,64},{64,80},{80,96},{96,112},{112,128},... | collective-permute-start | bytes 98312 | tf_op jit(solution)/shard_map/ppermute | solution.py:13
  11.4 5.8 %collective-permute-start.3 = (bf16[1,16,1024]{2,1,0:T(8,128)(2,1)S(1)}, bf16[1,16,1024]{2,1,0:T(8,128)(2,1)S(1)}, u32[]{:S(2)}, u32[]{:S(2)}) collective-permute-start(bf16[1,16,1024]{2,1,0:T(8,128)(2,1)S(1)} %slice.140), channel_id=1, source_target_pairs={{16,0},{32,16},{48,32},{64,48},{80,64},{96,80},{112,96},{128,112},... | collective-permute-start | bytes 98312 | tf_op jit(solution)/shard_map/ppermute | solution.py:16
  19.9 30.2 %copy-start.5 = (bf16[27,16,256]{2,1,0:T(8,128)(2,1)S(1)}, bf16[27,16,256]{2,1,0:T(8,128)(2,1)}, u32[]{:S(2)}) copy-start(bf16[27,16,256]{2,1,0:T(8,128)(2,1)} %param.4) | copy-start | bytes 663556
  22.5 18.2 %all-to-all-start.1 = ((bf16[16,2,3456]{2,1,0:T(2,128)(2,1)}), bf16[16,2,3456]{2,1,0:T(2,128)(2,1)S(1)}, u32[]{:S(2)}, u32[]{:S(2)}) async-start(bf16[16,2,3456]{2,1,0:T(2,128)(2,1)} %reshape.135), calls=%async_computation.1 | async-start | bytes 442368 | tf_op jit(solution)/shard_map/all_to_all | solution.py:45
  30.6 6.4 %collective-permute-start = (bf16[1,16,1024]{2,1,0:T(8,128)(2,1)S(1)}, bf16[1,16,1024]{2,1,0:T(8,128)(2,1)S(1)}, u32[]{:S(2)}, u32[]{:S(2)}) collective-permute-start(bf16[1,16,1024]{2,1,0:T(8,128)(2,1)S(1)} %slice.120), channel_id=1, source_target_pairs={{0,16},{16,32},{32,48},{48,64},{64,80},{80,96},{96,112},{112,128},... | collective-permute-start | bytes 98312 | tf_op jit(solution)/shard_map/ppermute | solution.py:13
  34.8 5.8 %collective-permute-start.1 = (bf16[1,16,1024]{2,1,0:T(8,128)(2,1)S(1)}, bf16[1,16,1024]{2,1,0:T(8,128)(2,1)S(1)}, u32[]{:S(2)}, u32[]{:S(2)}) collective-permute-start(bf16[1,16,1024]{2,1,0:T(8,128)(2,1)S(1)} %slice.122), channel_id=1, source_target_pairs={{16,0},{32,16},{48,32},{64,48},{80,64},{96,80},{112,96},{128,112},... | collective-permute-start | bytes 98312 | tf_op jit(solution)/shard_map/ppermute | solution.py:16
  40.7 11.6 %copy-start.6 = (bf16[16,2,3456]{2,1,0:T(2,128)(2,1)}, bf16[16,2,3456]{2,1,0:T(2,128)(2,1)S(1)}, u32[]{:S(2)}) copy-start(bf16[16,2,3456]{2,1,0:T(2,128)(2,1)S(1)} %all-to-all-done.1) | copy-start | bytes 663556
  42.2 39.5 %all-to-all-start = ((bf16[16,4,16,1024]{3,2,1,0:T(8,128)(2,1)}), bf16[16,4,16,1024]{3,2,1,0:T(8,128)(2,1)S(1)}, u32[]{:S(2)}, u32[]{:S(2)}) async-start(bf16[16,4,16,1024]{3,2,1,0:T(8,128)(2,1)} %stack.2), calls=%async_computation | async-start | bytes 4194304 | tf_op jit(solution)/shard_map/all_to_all | solution.py:50
  50.1 348.7 %all-reduce.4.cloned.1.call-start = ((), (), s32[]{:S(2)}) async-start(), calls=%async_computation.3 | async-start | bytes 1048576 | tf_op jit(solution)/shard_map/psum | solution.py:79
  81.7 1.3 copy-start.4
  84.8 8.0 %copy-start.10 = (bf16[1024]{0:T(1024)(128)(2,1)S(1)}, bf16[1024]{0:T(1024)(128)(2,1)}, u32[]{:S(2)}) copy-start(bf16[1024]{0:T(1024)(128)(2,1)} %fusion.75) | copy-start | bytes 6148
  89.8 2.5 copy-start.2
  95.9 6.5 %copy-start.3 = (bf16[4,2304,1024]{2,1,0:T(8,128)(2,1)}, bf16[4,2304,1024]{2,1,0:T(8,128)(2,1)S(1)}, u32[]{:S(2)}) copy-start(bf16[4,2304,1024]{2,1,0:T(8,128)(2,1)S(1)} %multiply_dynamic-update-slice_fusion) | copy-start | bytes 56623108
  120.4 6.4 %copy-start = (bf16[4,2304,1024]{2,1,0:T(8,128)(2,1)}, bf16[4,2304,1024]{2,1,0:T(8,128)(2,1)S(1)}, u32[]{:S(2)}) copy-start(bf16[4,2304,1024]{2,1,0:T(8,128)(2,1)S(1)} %fusion.27) | copy-start | bytes 56623108
  135.4 11.7 %copy-start.1 = (bf16[4,2304,1024]{2,1,0:T(8,128)(2,1)S(1)}, bf16[4,2304,1024]{2,1,0:T(8,128)(2,1)}, u32[]{:S(2)}) copy-start(bf16[4,2304,1024]{2,1,0:T(8,128)(2,1)} %copy-done) | copy-start | bytes 56623108
  140.6 6.7 %copy-start.7 = (bf16[16,2304,1]{1,0,2:T(8,128)(2,1)S(1)}, bf16[16,2304,1]{1,0,2:T(8,128)(2,1)}, u32[]{:S(2)}) copy-start(bf16[16,2304,1]{1,0,2:T(8,128)(2,1)} %reshape.121) | copy-start | bytes 221188
  147.2 1.3 copy-start.8
  148.6 1.4 copy-start.9
Sparse Core Ops, SparseCore 0:
  18.1 71.6 all-gather.1
  130.5 268.1 all-reduce.3
